TPU v7x, 32 devices: a whole 2x2x4 slice. The times are simulated.
32 devices in a mesh: group: 4 (over z), shard: 8 (over y, x, core).
Axes of the slice: x: 2, y: 2, z: 4, core: 2. Of those that a mesh axis runs over, the one named last changes fastest.
Arguments:
- query_hidden: bfloat16 [32, 32, 768], P(('group', 'shard')), may hold values from -6 to 6
- positive_hidden: bfloat16 [32, 64, 768], P(('group', 'shard')), may hold values from -6 to 6
- passage_store: bfloat16 [256, 64, 768], P('shard'), may hold values from -6 to 6
- negative_ids: int32 [32, 8], P(('group', 'shard')), may hold values from 0 to 255, as said below
- teacher_margins: int32 [32, 8], P(('group', 'shard')), may hold values from -4096 to 4095
- transform_weight: bfloat16 [768, 768], replicated, may hold values from -0.21875 to 0.21875
- vocab_weight: bfloat16 [768, 15360], P(None, 'shard'), may hold values from -0.21875 to 0.21875
- dense_weight: bfloat16 [768, 768], replicated, may hold values from -0.21875 to 0.21875
Outputs:
- student_margin: float32 [32, 8], P(('group', 'shard'))
- dense_grad: float32 [768, 768], replicated
Inputs may be any that keep to these rules, and one draw needn't show every extreme that they name: `negative_ids`: passage p is held by shard index p // 32. Among the 8 negatives of one index of group and shard, every store index is named by none or exactly 2 of them; one store index, drawn from the seed, is named 2 times by every index of group and shard.
All inputs are finite; a program needn't handle non-finite values.
Results may differ from a plain program's by a relative error of at most 0.0029.
Values may be sent and summed in bfloat16 or wider, within the bound.
A program may use at most 128 MiB of HBM per device.

v0:
```python
from functools import partial
import math
import jax
import jax.numpy as jnp
from jax import lax
from jax.sharding import PartitionSpec as P

CAP = 2


def encode(hidden, transform_weight):
    mixed_rows = jnp.dot(hidden, transform_weight, preferred_element_type=jnp.float32)
    active = jax.nn.gelu(mixed_rows, approximate=False)
    centre = jnp.mean(active, axis=-1, keepdims=True)
    spread = jnp.mean(jnp.square(active - centre), axis=-1, keepdims=True)
    return ((active - centre) * lax.rsqrt(spread + 1e-05)).astype(jnp.bfloat16)


def pool_single(sequence, vocab_weight):
    logits = jnp.dot(sequence, vocab_weight, preferred_element_type=jnp.float32)
    return jnp.max(jnp.log1p(jnp.maximum(logits, 0.0)), axis=0)


def pool_sequences(block_rows, offset, vocab_weight):
    return lax.map(partial(pool_single, vocab_weight=vocab_weight), block_rows, batch_size=8)


def add_outer(running, pieces):
    return running + jnp.einsum("rd,re->de", pieces[0], pieces[1], precision=lax.Precision.HIGHEST)


def body(
    query_hidden,
    positive_hidden,
    passage_store,
    negative_ids,
    teacher_margins,
    transform_weight,
    vocab_weight,
    dense_weight,
):
    shards = lax.axis_size("shard")
    queries_dev, negatives = negative_ids.shape
    store_rows, length, width = passage_store.shape
    vocab_total = vocab_weight.shape[1] * shards
    pooler = partial(pool_sequences, vocab_weight=vocab_weight)
    query_coded = encode(query_hidden, transform_weight)
    positive_coded = encode(positive_hidden, transform_weight)
    query_pool = pooler(lax.all_gather(query_coded, "shard", axis=0, tiled=True), jnp.int32(0))
    neg_total = queries_dev * negatives
    flat_ids = negative_ids.reshape(neg_total)
    owner_of = flat_ids // store_rows
    local_row = flat_ids % store_rows
    shard_ids = jnp.arange(shards, dtype=jnp.int32)
    owner_hit = (owner_of[:, None] == shard_ids[None, :]).astype(jnp.int32)
    earlier = jnp.cumsum(owner_hit, axis=0) - owner_hit
    slot_rank = jnp.sum(earlier * owner_hit, axis=1)
    slot_ids = jnp.arange(CAP, dtype=jnp.int32)
    slot_hit = (owner_hit[:, :, None] > 0) & (slot_rank[:, None, None] == slot_ids[None, None, :])
    asked_rows = jnp.sum(jnp.where(slot_hit, local_row[:, None, None], 0), axis=0)
    requests = jnp.where(jnp.any(slot_hit, axis=0), asked_rows, -1)
    asked_for = lax.all_to_all(requests, "shard", split_axis=0, concat_axis=0, tiled=True)
    is_valid = asked_for >= 0
    served = passage_store[jnp.clip(asked_for, 0, store_rows - 1)]
    served = jnp.where(is_valid[:, :, None, None], served, jnp.zeros((), served.dtype))
    fetched = lax.all_to_all(served, "shard", split_axis=0, concat_axis=0, tiled=True)
    negative_hidden = fetched.reshape(shards * CAP, length, width)[owner_of * CAP + slot_rank]
    negative_coded = encode(negative_hidden, transform_weight)
    passages = jnp.concatenate(
        [positive_coded[:, None], negative_coded.reshape(queries_dev, negatives, length, width)],
        axis=1,
    )
    passages = passages.reshape(queries_dev * (1 + negatives), length, width)
    passage_pool = pooler(lax.all_gather(passages, "shard", axis=0, tiled=True), jnp.int32(0))
    passage_pool = passage_pool.reshape(shards * queries_dev, 1 + negatives, -1)
    pair_terms = jnp.einsum("qv,qjv->qj", query_pool, passage_pool, precision=lax.Precision.HIGHEST)
    sparse = lax.psum_scatter(pair_terms, "shard", scatter_dimension=0, tiled=True) / math.sqrt(
        vocab_total
    )
    inv_root = 1.0 / math.sqrt(width)
    query_cls = query_hidden[:, 0, :]
    positive_cls = positive_hidden[:, 0, :]
    negative_cls = negative_hidden[:, 0, :].reshape(queries_dev, negatives, width)
    query_vec = jnp.dot(query_cls, dense_weight, preferred_element_type=jnp.float32)
    positive_vec = jnp.dot(positive_cls, dense_weight, preferred_element_type=jnp.float32)
    negative_vec = jnp.dot(negative_cls, dense_weight, preferred_element_type=jnp.float32)
    dense_pos = jnp.sum(query_vec * positive_vec, axis=1) * inv_root
    dense_neg = (
        jnp.einsum("qd,qkd->qk", query_vec, negative_vec, precision=lax.Precision.HIGHEST)
        * inv_root
    )
    pos_score = sparse[:, 0] + dense_pos
    neg_score = sparse[:, 1:] + dense_neg
    margin = pos_score[:, None] - neg_score
    target = teacher_margins.astype(jnp.float32) / 1024.0
    coef = (margin - target) / negatives
    coef_total = jnp.sum(coef, axis=1)
    grad_query = (
        coef_total[:, None] * positive_vec
        - jnp.einsum("qk,qkd->qd", coef, negative_vec, precision=lax.Precision.HIGHEST)
    ) * inv_root
    grad_positive = coef_total[:, None] * query_vec * inv_root
    grad_negative = -coef[:, :, None] * query_vec[:, None, :] * inv_root
    states = jnp.concatenate(
        [query_cls, positive_cls, negative_cls.reshape(-1, width)], axis=0
    ).astype(jnp.float32)
    factors = jnp.concatenate([grad_query, grad_positive, grad_negative.reshape(-1, width)], axis=0)
    empty = jnp.zeros((width, width), jnp.float32)
    dense_grad = add_outer(
        empty,
        (
            lax.all_gather(states, ("group", "shard"), axis=0, tiled=True),
            lax.all_gather(factors, ("group", "shard"), axis=0, tiled=True),
        ),
    )
    return (margin, dense_grad)


def solution(mesh):
    in_specs = (
        P(("group", "shard"), None, None),
        P(("group", "shard"), None, None),
        P("shard", None, None),
        P(("group", "shard"), None),
        P(("group", "shard"), None),
        P(),
        P(None, "shard"),
        P(),
    )
    out_specs = (P(("group", "shard"), None), P())
    return jax.shard_map(body, mesh=mesh, in_specs=in_specs, out_specs=out_specs, check_vma=False)
```

profile of v0, /device:TPU:0, one launch (start us, length us, event | category | flops | bytes accessed | tf_op | source)
XLA Modules:
  0.0 263.6 jit_solution(15380211158896153419)
XLA Ops:
  7.2 0.8 and_select_fusion.2
  8.1 0.2 select_reduce_fusion
  8.3 0.1 and_reduce_fusion
  8.4 0.1 fusion.63
  8.5 0.1 copy.29
  8.6 9.7 %all_to_all.11 = s32[8,1,2]{2,1,0:T(1,128)S(1)} all-to-all(s32[8,1,2]{2,1,0:T(1,128)S(1)} %copy.29), channel_id=1, replica_groups=mesh['group'=4,'shard'=8] {'shard'}, dimensions={0} | all-to-all | bytes 128 | tf_op jit(solution)/shard_map/all_to_all | solution.py:62
  18.4 0.1 reshape.525
  18.5 0.1 copy.31
  18.6 1.8 gather_fusion
  20.4 2.7 %broadcast_select_fusion = bf16[8,2,64,768]{3,2,1,0:T(8,128)(2,1)} fusion(bf16[8,2,64,768]{3,2,1,0:T(8,128)(2,1)} %bitcast.160, pred[8,2]{1,0:T(8,128)(4,1)S(1)} %copy.31), kind=kLoop, calls=%fused_computation.37 | loop fusion | flops 786432 | bytes 3145744 | tf_op jit(solution)/shard_map/jit(_where)/select_n | solution.py:65
  23.1 4.4 %all-to-all-start.1 = ((bf16[8,2,64,768]{3,2,1,0:T(8,128)(2,1)}), bf16[8,2,64,768]{3,2,1,0:T(8,128)(2,1)}, u32[]{:S(2)}, u32[]{:S(2)}) async-start(bf16[8,2,64,768]{3,2,1,0:T(8,128)(2,1)} %broadcast_select_fusion), calls=%async_computation.1 | async-start | bytes 3145728 | tf_op jit(solution)/shard_map/all_to_all | solution.py:66
  27.7 2.0 fusion.77
  29.7 0.2 multiply_reduce_fusion.1
  29.9 0.1 fusion.44
  30.0 18.5 %all-to-all-done.1 = bf16[8,2,64,768]{3,2,1,0:T(8,128)(2,1)} async-done(((bf16[8,2,64,768]{3,2,1,0:T(8,128)(2,1)}), bf16[8,2,64,768]{3,2,1,0:T(8,128)(2,1)}, u32[]{:S(2)}, u32[]{:S(2)}) %all-to-all-start.1) | async-done | bytes 1572896 | tf_op jit(solution)/shard_map/all_to_all | solution.py:66
  48.6 2.9 %gather_fusion.1 = bf16[8,64,768]{2,1,0:T(8,128)(2,1)} fusion(bf16[16,64,768]{2,1,0:T(8,128)(2,1)} %bitcast.14, s32[1024]{0:T(1024)S(1)} %pad_clamp_fusion), kind=kCustom, calls=%fused_computation.1 | custom fusion | bytes 1572896 | tf_op jit(solution)/shard_map/gather | solution.py:67
  51.4 2.8 %fusion.31 = (u8[64,768]{1,0:T(8,128)(4,1)S(1)}, u8[64,768]{1,0:T(8,128)(4,1)S(1)}, u8[64,768]{1,0:T(8,128)(4,1)S(1)}, f32[8,64,768]{2,1,0:T(8,128)S(1)}) fusion(bf16[8,64,768]{2,1,0:T(8,128)(2,1)} %gather_fusion.1, bf16[768,768]{1,0:T(8,128)(2,1)} %param.15), kind=kOutput, calls=%fused_computation.51 | convolution fusion | flops 611696640 | bytes 3686400 | tf_op jit(solution)/shard_map/dot_general | solution.py:12
  54.3 3.8 %fusion.75 = (f32[8,64]{1,0:T(8,128)S(1)}, f32[8,64,768]{2,1,0:T(8,128)S(1)}) fusion(u8[64,768]{1,0:T(8,128)(4,1)S(1)} %get-tuple-element.38, u8[64,768]{1,0:T(8,128)(4,1)S(1)} %get-tuple-element.39, f32[8,64,768]{2,1,0:T(8,128)S(1)} %get-tuple-element.56, u8[64,768]{1,0:T(8,128)(4,1)S(1)} %get-tuple-element.37), kind=kLoop, calls=%fused_computation.154 | loop fusion | flops 28311040 | bytes 3295232 | tf_op jit(solution)/shard_map/reduce_sum | solution.py:14
  58.1 0.3 multiply_reduce_fusion
  58.5 0.2 fusion.29
  58.7 1.0 maximum_bitcast_fusion
  59.8 0.7 dynamic-slice.1
  60.4 1.6 convolution_reduce_fusion.1
  62.0 1.6 fusion.79
  63.5 0.7 multiply_reduce_fusion.3
  64.9 2.1 fusion.78
  67.0 0.2 multiply_reduce_fusion.2
  67.2 0.1 multiply_convert_fusion.2
  67.3 10.4 %all-gather = bf16[256,768]{1,0:T(8,128)(2,1)S(1)} all-gather(bf16[32,768]{1,0:T(8,128)(2,1)S(1)} %multiply_convert_fusion.2), channel_id=2, replica_groups=mesh['group'=4,'shard'=8] {'shard'}, dimensions={0}, use_global_device_ids=true | all-gather | bytes 442368 | tf_op jit(solution)/shard_map/all_gather | solution.py:49
  77.8 1.4 fusion.20
  79.2 0.9 slice.24
  80.1 50.6 %all-gather.2 = f32[32,10,768]{2,1,0:T(8,128)} all-gather(f32[1,10,768]{2,1,0:T(8,128)S(1)} %fusion.62), channel_id=1, replica_groups=mesh['group'=4,'shard'=8] {'group','shard'}, dimensions={0}, use_global_device_ids=true | all-gather | bytes 1013760 | tf_op jit(solution)/shard_map/all_gather | solution.py:112
  130.8 2.5 reshape.544
  133.3 1.5 fusion.80
  134.8 48.1 %while.2 = (s32[]{:T(128)}, f32[9,8,1920]{2,1,0:T(8,128)}, bf16[9,8,64,768]{3,2,1,0:T(8,128)(2,1)}, bf16[768,1920]{1,0:T(8,128)(2,1)}, s32[]{:T(128)}) while((s32[]{:T(128)}, f32[9,8,1920]{2,1,0:T(8,128)}, bf16[9,8,64,768]{3,2,1,0:T(8,128)(2,1)}, bf16[768,1920]{1,0:T(8,128)(2,1)}, s32[]{:T(128)}) %tuple.40), condition=%wide.region_13.14_spmd, body=%wide.region_11.13_spmd.sunk | while | flops 1511900160 | bytes 3919949 | solution.py:25
  134.8 4.7 %log-plus-one_reduce_fusion.2 = f32[8,1920]{1,0:T(8,128)S(1)} fusion(bf16[768,1920]{1,0:T(8,128)(2,1)} %get-tuple-element.102, bf16[9,8,64,768]{3,2,1,0:T(8,128)(2,1)} %get-tuple-element.101, s32[]{:T(128)S(6)} %copy.45), kind=kOutput, calls=%fused_computation.2.clone.1 | convolution fusion | flops 1511900160 | bytes 3796996 | tf_op jit(solution)/shard_map/while/body/eval_jaxpr/vmap()/dot_general | solution.py:20
  139.6 0.6 bitcast_dynamic-update-slice_fusion.2
  140.2 4.7 %log-plus-one_reduce_fusion.2 = f32[8,1920]{1,0:T(8,128)S(1)} fusion(bf16[768,1920]{1,0:T(8,128)(2,1)} %get-tuple-element.102, bf16[9,8,64,768]{3,2,1,0:T(8,128)(2,1)} %get-tuple-element.101, s32[]{:T(128)S(6)} %copy.45), kind=kOutput, calls=%fused_computation.2.clone.1 | convolution fusion | flops 1511900160 | bytes 3796996 | tf_op jit(solution)/shard_map/while/body/eval_jaxpr/vmap()/dot_general | solution.py:20
  144.9 0.6 bitcast_dynamic-update-slice_fusion.2
  145.5 4.7 %log-plus-one_reduce_fusion.2 = f32[8,1920]{1,0:T(8,128)S(1)} fusion(bf16[768,1920]{1,0:T(8,128)(2,1)} %get-tuple-element.102, bf16[9,8,64,768]{3,2,1,0:T(8,128)(2,1)} %get-tuple-element.101, s32[]{:T(128)S(6)} %copy.45), kind=kOutput, calls=%fused_computation.2.clone.1 | convolution fusion | flops 1511900160 | bytes 3796996 | tf_op jit(solution)/shard_map/while/body/eval_jaxpr/vmap()/dot_general | solution.py:20
  150.3 0.6 bitcast_dynamic-update-slice_fusion.2
  150.9 4.7 %log-plus-one_reduce_fusion.2 = f32[8,1920]{1,0:T(8,128)S(1)} fusion(bf16[768,1920]{1,0:T(8,128)(2,1)} %get-tuple-element.102, bf16[9,8,64,768]{3,2,1,0:T(8,128)(2,1)} %get-tuple-element.101, s32[]{:T(128)S(6)} %copy.45), kind=kOutput, calls=%fused_computation.2.clone.1 | convolution fusion | flops 1511900160 | bytes 3796996 | tf_op jit(solution)/shard_map/while/body/eval_jaxpr/vmap()/dot_general | solution.py:20
  155.6 0.6 bitcast_dynamic-update-slice_fusion.2
  156.2 4.7 %log-plus-one_reduce_fusion.2 = f32[8,1920]{1,0:T(8,128)S(1)} fusion(bf16[768,1920]{1,0:T(8,128)(2,1)} %get-tuple-element.102, bf16[9,8,64,768]{3,2,1,0:T(8,128)(2,1)} %get-tuple-element.101, s32[]{:T(128)S(6)} %copy.45), kind=kOutput, calls=%fused_computation.2.clone.1 | convolution fusion | flops 1511900160 | bytes 3796996 | tf_op jit(solution)/shard_map/while/body/eval_jaxpr/vmap()/dot_general | solution.py:20
  160.9 0.6 bitcast_dynamic-update-slice_fusion.2
  161.6 4.7 %log-plus-one_reduce_fusion.2 = f32[8,1920]{1,0:T(8,128)S(1)} fusion(bf16[768,1920]{1,0:T(8,128)(2,1)} %get-tuple-element.102, bf16[9,8,64,768]{3,2,1,0:T(8,128)(2,1)} %get-tuple-element.101, s32[]{:T(128)S(6)} %copy.45), kind=kOutput, calls=%fused_computation.2.clone.1 | convolution fusion | flops 1511900160 | bytes 3796996 | tf_op jit(solution)/shard_map/while/body/eval_jaxpr/vmap()/dot_general | solution.py:20
  166.3 0.6 bitcast_dynamic-update-slice_fusion.2
  166.9 4.7 %log-plus-one_reduce_fusion.2 = f32[8,1920]{1,0:T(8,128)S(1)} fusion(bf16[768,1920]{1,0:T(8,128)(2,1)} %get-tuple-element.102, bf16[9,8,64,768]{3,2,1,0:T(8,128)(2,1)} %get-tuple-element.101, s32[]{:T(128)S(6)} %copy.45), kind=kOutput, calls=%fused_computation.2.clone.1 | convolution fusion | flops 1511900160 | bytes 3796996 | tf_op jit(solution)/shard_map/while/body/eval_jaxpr/vmap()/dot_general | solution.py:20
  171.6 0.6 bitcast_dynamic-update-slice_fusion.2
  172.3 4.7 %log-plus-one_reduce_fusion.2 = f32[8,1920]{1,0:T(8,128)S(1)} fusion(bf16[768,1920]{1,0:T(8,128)(2,1)} %get-tuple-element.102, bf16[9,8,64,768]{3,2,1,0:T(8,128)(2,1)} %get-tuple-element.101, s32[]{:T(128)S(6)} %copy.45), kind=kOutput, calls=%fused_computation.2.clone.1 | convolution fusion | flops 1511900160 | bytes 3796996 | tf_op jit(solution)/shard_map/while/body/eval_jaxpr/vmap()/dot_general | solution.py:20
  177.0 0.6 bitcast_dynamic-update-slice_fusion.2
  177.6 4.7 %log-plus-one_reduce_fusion.2 = f32[8,1920]{1,0:T(8,128)S(1)} fusion(bf16[768,1920]{1,0:T(8,128)(2,1)} %get-tuple-element.102, bf16[9,8,64,768]{3,2,1,0:T(8,128)(2,1)} %get-tuple-element.101, s32[]{:T(128)S(6)} %copy.45), kind=kOutput, calls=%fused_computation.2.clone.1 | convolution fusion | flops 1511900160 | bytes 3796996 | tf_op jit(solution)/shard_map/while/body/eval_jaxpr/vmap()/dot_general | solution.py:20
  182.3 0.6 bitcast_dynamic-update-slice_fusion.2
  182.9 2.1 reshape_reshape.3
  185.0 2.5 fusion.56
  187.5 12.1 %all-reduce = f32[8,9]{1,0:T(8,128)S(1)} all-reduce(f32[8,9]{1,0:T(8,128)S(1)} %bitcast.165), channel_id=4, replica_groups=mesh['group'=4,'shard'=8] {'shard'}, use_global_device_ids=true, to_apply=%region_14.15.clone | all-reduce | flops 72 | bytes 576
  199.6 0.6 dynamic-slice_multiply_fusion
  200.3 1.4 fusion.74
  201.7 0.2 convolution_reduce_fusion
  201.9 0.7 multiply_multiply_fusion.16
  202.6 0.7 subtract_multiply_fusion
  203.4 44.1 %all-gather.3 = f32[32,10,768]{2,1,0:T(8,128)} all-gather(f32[1,10,768]{2,1,0:T(8,128)S(1)} %maximum_bitcast_fusion.1), channel_id=1, replica_groups=mesh['group'=4,'shard'=8] {'group','shard'}, dimensions={0}, use_global_device_ids=true | all-gather | bytes 1013760 | tf_op jit(solution)/shard_map/all_gather | solution.py:113
  247.5 2.4 reshape.546
  249.9 6.9 %fusion.81 = f32[768,768]{1,0:T(8,128)} fusion(f32[320,768]{1,0:T(8,128)} %reshape.544, f32[320,768]{1,0:T(8,128)} %reshape.546), kind=kOutput, calls=%fused_computation.159 | convolution fusion | flops 2264924160 | bytes 4325376 | tf_op jit(solution)/shard_map/rd,re->de/dot_general | solution.py:29
  (44 shorter events, 0.6 us)
Async XLA Ops:
  7.2 11.4 %copy-start = (bf16[32,64,768]{2,1,0:T(8,128)(2,1)S(1)}, bf16[32,64,768]{2,1,0:T(8,128)(2,1)}, u32[]{:S(2)}) copy-start(bf16[32,64,768]{2,1,0:T(8,128)(2,1)} %param.12) | copy-start | bytes 9437188
  23.1 4.5 %copy-start.5 = (s32[1,8]{1,0:T(1,128)S(1)}, s32[1,8]{1,0:T(1,128)}, u32[]{:S(2)}) copy-start(s32[1,8]{1,0:T(1,128)} %param.13) | copy-start | bytes 100
  23.1 4.5 %copy-start.2 = (bf16[1,64,768]{2,1,0:T(8,128)(2,1)S(1)}, bf16[1,64,768]{2,1,0:T(8,128)(2,1)}, u32[]{:S(2)}) copy-start(bf16[1,64,768]{2,1,0:T(8,128)(2,1)} %param.11) | copy-start | bytes 294916
  23.1 25.4 %all-to-all-start.1 = ((bf16[8,2,64,768]{3,2,1,0:T(8,128)(2,1)}), bf16[8,2,64,768]{3,2,1,0:T(8,128)(2,1)}, u32[]{:S(2)}, u32[]{:S(2)}) async-start(bf16[8,2,64,768]{3,2,1,0:T(8,128)(2,1)} %broadcast_select_fusion), calls=%async_computation.1 | async-start | bytes 3145728 | tf_op jit(solution)/shard_map/all_to_all | solution.py:66
  27.6 107.3 %all-gather.6.cloned.1.call-start = ((), (), s32[]{:S(2)}) async-start(), calls=%async_computation.2 | async-start | bytes 7962624 | tf_op jit(solution)/shard_map/all_gather | solution.py:74
  58.7 1.1 copy-start.6
  58.7 3.3 %copy-start.1 = (bf16[1,32,768]{2,1,0:T(8,128)(2,1)S(1)}, bf16[1,32,768]{2,1,0:T(8,128)(2,1)}, u32[]{:S(2)}) copy-start(bf16[1,32,768]{2,1,0:T(8,128)(2,1)} %param.10) | copy-start | bytes 147460
  64.9 12.8 %copy-start.4 = (bf16[768,1920]{1,0:T(8,128)(2,1)S(1)}, bf16[768,1920]{1,0:T(8,128)(2,1)}, u32[]{:S(2)}) copy-start(bf16[768,1920]{1,0:T(8,128)(2,1)} %param.16) | copy-start | bytes 8847364
  182.9 17.4 %copy-start.3 = (s32[1,8]{1,0:T(1,128)S(1)}, s32[1,8]{1,0:T(1,128)}, u32[]{:S(2)}) copy-start(s32[1,8]{1,0:T(1,128)} %param.14) | copy-start | bytes 100
Sparse Core Ops, SparseCore 0:
  59.9 59.8 all-gather.5
where the time goes:
time: 264 us
  blocking collectives  127 us (48%)
  matrix products  66.2 us (25%)
  local copies, waits for them, and re-layouts  19.4 us (7%)
  waiting for transfers between devices  18.6 us (7%)
  between operations  15.1 us (6%)
  other arithmetic  12.9 us (5%)
  starting transfers between devices  4.46 us (2%)
    all_gather x1, blocking collectives, body(): lax.all_gather(states, ('group', 'shard'), axis=0, tiled=True)  50.6 us
    all_gather x1, blocking collectives, body(): lax.all_gather(factors, ('group', 'shard'), axis=0, tiled=True)  44.1 us
    dot_general x10, matrix products, pool_single(): logits = jnp.dot(sequence, vocab_weight, preferred_element_type=jnp.float32)  43.8 us
    all_to_all x1, waiting for transfers between devices, body(): lax.all_to_all(served, 'shard', split_axis=0, concat_axis=0, tiled=True)  18.5 us
    unnamed x1, blocking collectives  12.1 us
    all_gather x1, blocking collectives, body(): lax.all_gather(query_coded, 'shard', axis=0, tiled=True)  10.4 us
    all_to_all x1, blocking collectives, body(): lax.all_to_all(requests, 'shard', split_axis=0, concat_axis=0, tiled=True)  9.68 us
    dot_general x3, matrix products, encode(): jnp.dot(hidden, transform_weight, preferred_element_type=jnp.float32)  6.94 us
  transfers between devices with their start and end apart: 2, of which 1 were waited for; matrix products, arithmetic and copies ran while one was open for 6% of the time, Pallas kernels for 0%

commit v1 on v0

--- a/solution.py
+++ b/solution.py
@@ -63,7 +63,19 @@
     is_valid = asked_for >= 0
     served = passage_store[jnp.clip(asked_for, 0, store_rows - 1)]
     served = jnp.where(is_valid[:, :, None, None], served, jnp.zeros((), served.dtype))
-    fetched = lax.all_to_all(served, "shard", split_axis=0, concat_axis=0, tiled=True)
+    ways, here = (lax.axis_size("shard"), lax.axis_index("shard"))
+    width_2 = served.shape[0] // ways
+    dims = list(served.shape)
+    dims[0] = width_2
+    height = dims[0]
+    dims[0] = height * ways
+    full = jnp.zeros(dims, served.dtype)
+    for mask in range(ways):
+        part = lax.dynamic_slice_in_dim(served, (here ^ mask) * width_2, width_2, axis=0)
+        if mask:
+            part = lax.ppermute(part, "shard", [(d, d ^ mask) for d in range(ways)])
+        full = lax.dynamic_update_slice_in_dim(full, part, (here ^ mask) * height, axis=0)
+    fetched = full
     negative_hidden = fetched.reshape(shards * CAP, length, width)[owner_of * CAP + slot_rank]
     negative_coded = encode(negative_hidden, transform_weight)
     passages = jnp.concatenate(

time: 264 us -> 265 us (level)
  blocking collectives: 127 us -> 118 us
  local copies, waits for them, and re-layouts: 19.4 us -> 27.6 us
  starting transfers between devices: 4.46 us -> 9.69 us
  waiting for transfers between devices: 18.6 us -> 15.8 us
    all_to_all x1, waiting for transfers between devices: 18.5 us -> 2.08 us  [body(): lax.all_to_all(requests, 'shard', split_axis=0, concat_axis=0, tiled=True)]
    ppermute x0 -> x7, waiting for transfers between devices: none -> 13.7 us  [body(): part = lax.ppermute(part, 'shard', [(d, d ^ mask) for d in range(ways)])]
    all_to_all x1 -> x0, blocking collectives: 9.68 us -> none  [body(): lax.all_to_all(requests, 'shard', split_axis=0, concat_axis=0, tiled=True)]
    dynamic_update_slice x0 -> x7, local copies, waits for them, and re-layouts: none -> 4.83 us  [body(): lax.dynamic_update_slice_in_dim(full, part, (here ^ mask) * height, axis=0)]
    ppermute x0 -> x7, starting transfers between devices: none -> 4.46 us  [body(): part = lax.ppermute(part, 'shard', [(d, d ^ mask) for d in range(ways)])]
    unnamed x18 -> x16, local copies, waits for them, and re-layouts: 5.61 us -> 5.6 us
  transfers between devices with their start and end apart: 2 -> 9, of which waited for: 1 -> 4; matrix products, arithmetic and copies ran while one was open for 6% -> 8% of each run, Pallas kernels for 0% -> 0%
where the time goes in v1:
time: 265 us; the launch traced here: 264 us
  blocking collectives  118 us (45%)
  matrix products  66.3 us (25%)
  local copies, waits for them, and re-layouts  27.6 us (10%)
  waiting for transfers between devices  15.8 us (6%)
  between operations  15.1 us (6%)
  other arithmetic  11.7 us (4%)
  starting transfers between devices  9.69 us (4%)
    all_gather x1, blocking collectives, body(): lax.all_gather(states, ('group', 'shard'), axis=0, tiled=True)  51.1 us
    all_gather x1, blocking collectives, body(): lax.all_gather(factors, ('group', 'shard'), axis=0, tiled=True)  43.9 us
    dot_general x10, matrix products, pool_single(): logits = jnp.dot(sequence, vocab_weight, preferred_element_type=jnp.float32)  43.8 us
    ppermute x7, waiting for transfers between devices, body(): part = lax.ppermute(part, 'shard', [(d, d ^ mask) for d in range(ways)])  13.7 us
    unnamed x1, blocking collectives  12.1 us
    all_gather x1, blocking collectives, body(): lax.all_gather(query_coded, 'shard', axis=0, tiled=True)  10.6 us
    dot_general x3, matrix products, encode(): jnp.dot(hidden, transform_weight, preferred_element_type=jnp.float32)  6.99 us
    dot_general x1, matrix products, add_outer(): jnp.einsum('rd,re->de', pieces[0], pieces[1], precision=lax.Precision.HIG...  6.86 us
  transfers between devices with their start and end apart: 9, of which 4 were waited for; matrix products, arithmetic and copies ran while one was open for 8% of the time, Pallas kernels for 0%

profile of v1, /device:TPU:0, one launch (start us, length us, event | category | flops | bytes accessed | tf_op | source)
XLA Modules:
  0.0 264.0 jit_solution(4247980752473183695)
XLA Ops:
  7.2 0.8 and_select_fusion.2
  8.5 0.7 copy.29
  9.2 5.2 %all-to-all-start = ((s32[8,1,2]{2,1,0:T(1,128)}), s32[8,1,2]{2,1,0:T(1,128)S(1)}, u32[]{:S(2)}, u32[]{:S(2)}) async-start(s32[8,1,2]{2,1,0:T(1,128)} %copy.29), calls=%async_computation | async-start | bytes 8192 | tf_op jit(solution)/shard_map/all_to_all | solution.py:62
  14.4 2.1 fusion.77
  16.9 2.1 all-to-all-done
  19.3 1.8 gather_fusion
  21.1 1.6 broadcast_select_fusion
  22.7 1.3 broadcast_in_dim.41
  24.0 0.8 constant_dynamic-slice_fusion
  25.5 1.3 collective-permute-start.2
  27.3 1.1 collective-permute-start.4
  28.4 0.9 collective-permute-start.5
  29.3 0.7 constant_dynamic-update-slice_fusion.6
  30.0 2.7 %collective-permute-done.1 = bf16[1,2,64,768]{3,2,1,0:T(8,128)(2,1)S(1)} collective-permute-done((bf16[1,2,64,768]{3,2,1,0:T(8,128)(2,1)S(1)}, bf16[1,2,64,768]{3,2,1,0:T(8,128)(2,1)S(1)}, u32[]{:S(2)}, u32[]{:S(2)}) %collective-permute-start.1) | collective-permute-done | bytes 196640 | tf_op jit(solution)/shard_map/ppermute | solution.py:76
  32.7 0.7 constant_dynamic-update-slice_fusion.5
  33.4 2.6 collective-permute-done.2
  36.0 0.7 constant_dynamic-update-slice_fusion.4
  36.7 0.7 constant_dynamic-update-slice_fusion.3
  37.4 8.5 %collective-permute-done.4 = bf16[1,2,64,768]{3,2,1,0:T(8,128)(2,1)S(1)} collective-permute-done((bf16[1,2,64,768]{3,2,1,0:T(8,128)(2,1)S(1)}, bf16[1,2,64,768]{3,2,1,0:T(8,128)(2,1)S(1)}, u32[]{:S(2)}, u32[]{:S(2)}) %collective-permute-start.4) | collective-permute-done | bytes 196640 | tf_op jit(solution)/shard_map/ppermute | solution.py:76
  45.8 0.7 constant_dynamic-update-slice_fusion.2
  46.5 0.7 constant_dynamic-update-slice_fusion.1
  47.2 0.7 constant_dynamic-update-slice_fusion
  47.9 2.9 %gather_fusion.1 = bf16[8,64,768]{2,1,0:T(8,128)(2,1)} fusion(bf16[16,64,768]{2,1,0:T(8,128)(2,1)} %bitcast.14, s32[1024]{0:T(1024)S(1)} %pad_clamp_fusion), kind=kCustom, calls=%fused_computation.1 | custom fusion | bytes 1572896 | tf_op jit(solution)/shard_map/gather | solution.py:79
  50.8 2.8 %fusion.31 = (u8[64,768]{1,0:T(8,128)(4,1)S(1)}, u8[64,768]{1,0:T(8,128)(4,1)S(1)}, u8[64,768]{1,0:T(8,128)(4,1)S(1)}, f32[8,64,768]{2,1,0:T(8,128)S(1)}) fusion(bf16[8,64,768]{2,1,0:T(8,128)(2,1)} %gather_fusion.1, bf16[768,768]{1,0:T(8,128)(2,1)} %param.15), kind=kOutput, calls=%fused_computation.51 | convolution fusion | flops 611696640 | bytes 3686400 | tf_op jit(solution)/shard_map/dot_general | solution.py:12
  53.6 3.8 %fusion.75 = (f32[8,64]{1,0:T(8,128)S(1)}, f32[8,64,768]{2,1,0:T(8,128)S(1)}) fusion(u8[64,768]{1,0:T(8,128)(4,1)S(1)} %get-tuple-element.38, u8[64,768]{1,0:T(8,128)(4,1)S(1)} %get-tuple-element.39, f32[8,64,768]{2,1,0:T(8,128)S(1)} %get-tuple-element.64, u8[64,768]{1,0:T(8,128)(4,1)S(1)} %get-tuple-element.37), kind=kLoop, calls=%fused_computation.169 | loop fusion | flops 28311040 | bytes 3295232 | tf_op jit(solution)/shard_map/reduce_sum | solution.py:14
  58.0 1.0 maximum_bitcast_fusion
  59.1 0.7 dynamic-slice.1
  59.7 1.6 convolution_reduce_fusion.1
  61.3 1.6 fusion.79
  62.9 0.7 multiply_reduce_fusion.3
  64.3 2.1 fusion.78
  66.7 10.6 %all-gather = bf16[256,768]{1,0:T(8,128)(2,1)S(1)} all-gather(bf16[32,768]{1,0:T(8,128)(2,1)S(1)} %multiply_convert_fusion.2), channel_id=2, replica_groups=mesh['group'=4,'shard'=8] {'shard'}, dimensions={0}, use_global_device_ids=true | all-gather | bytes 442368 | tf_op jit(solution)/shard_map/all_gather | solution.py:49
  77.2 0.7 slice_bitcast_fusion
  78.0 1.4 fusion.20
  79.4 0.9 slice.24
  80.3 51.1 %all-gather.2 = f32[32,10,768]{2,1,0:T(8,128)} all-gather(f32[1,10,768]{2,1,0:T(8,128)S(1)} %fusion.62), channel_id=1, replica_groups=mesh['group'=4,'shard'=8] {'group','shard'}, dimensions={0}, use_global_device_ids=true | all-gather | bytes 1013760 | tf_op jit(solution)/shard_map/all_gather | solution.py:124
  131.4 2.5 reshape.544
  133.9 1.5 fusion.80
  135.5 48.1 %while.2 = (s32[]{:T(128)}, f32[9,8,1920]{2,1,0:T(8,128)}, bf16[9,8,64,768]{3,2,1,0:T(8,128)(2,1)}, bf16[768,1920]{1,0:T(8,128)(2,1)}, s32[]{:T(128)}) while((s32[]{:T(128)}, f32[9,8,1920]{2,1,0:T(8,128)}, bf16[9,8,64,768]{3,2,1,0:T(8,128)(2,1)}, bf16[768,1920]{1,0:T(8,128)(2,1)}, s32[]{:T(128)}) %tuple.47), condition=%wide.region_13.14_spmd, body=%wide.region_11.13_spmd.sunk | while | flops 1511900160 | bytes 3919949 | solution.py:25
  135.5 4.7 %log-plus-one_reduce_fusion.2 = f32[8,1920]{1,0:T(8,128)S(1)} fusion(bf16[768,1920]{1,0:T(8,128)(2,1)} %get-tuple-element.110, bf16[9,8,64,768]{3,2,1,0:T(8,128)(2,1)} %get-tuple-element.109, s32[]{:T(128)S(6)} %copy.53), kind=kOutput, calls=%fused_computation.2.clone.1 | convolution fusion | flops 1511900160 | bytes 3796996 | tf_op jit(solution)/shard_map/while/body/eval_jaxpr/vmap()/dot_general | solution.py:20
  140.8 4.7 %log-plus-one_reduce_fusion.2 = f32[8,1920]{1,0:T(8,128)S(1)} fusion(bf16[768,1920]{1,0:T(8,128)(2,1)} %get-tuple-element.110, bf16[9,8,64,768]{3,2,1,0:T(8,128)(2,1)} %get-tuple-element.109, s32[]{:T(128)S(6)} %copy.53), kind=kOutput, calls=%fused_computation.2.clone.1 | convolution fusion | flops 1511900160 | bytes 3796996 | tf_op jit(solution)/shard_map/while/body/eval_jaxpr/vmap()/dot_general | solution.py:20
  145.5 0.6 bitcast_dynamic-update-slice_fusion.2
  146.2 4.7 %log-plus-one_reduce_fusion.2 = f32[8,1920]{1,0:T(8,128)S(1)} fusion(bf16[768,1920]{1,0:T(8,128)(2,1)} %get-tuple-element.110, bf16[9,8,64,768]{3,2,1,0:T(8,128)(2,1)} %get-tuple-element.109, s32[]{:T(128)S(6)} %copy.53), kind=kOutput, calls=%fused_computation.2.clone.1 | convolution fusion | flops 1511900160 | bytes 3796996 | tf_op jit(solution)/shard_map/while/body/eval_jaxpr/vmap()/dot_general | solution.py:20
  150.9 0.6 bitcast_dynamic-update-slice_fusion.2
  151.5 4.7 %log-plus-one_reduce_fusion.2 = f32[8,1920]{1,0:T(8,128)S(1)} fusion(bf16[768,1920]{1,0:T(8,128)(2,1)} %get-tuple-element.110, bf16[9,8,64,768]{3,2,1,0:T(8,128)(2,1)} %get-tuple-element.109, s32[]{:T(128)S(6)} %copy.53), kind=kOutput, calls=%fused_computation.2.clone.1 | convolution fusion | flops 1511900160 | bytes 3796996 | tf_op jit(solution)/shard_map/while/body/eval_jaxpr/vmap()/dot_general | solution.py:20
  156.2 0.6 bitcast_dynamic-update-slice_fusion.2
  156.9 4.7 %log-plus-one_reduce_fusion.2 = f32[8,1920]{1,0:T(8,128)S(1)} fusion(bf16[768,1920]{1,0:T(8,128)(2,1)} %get-tuple-element.110, bf16[9,8,64,768]{3,2,1,0:T(8,128)(2,1)} %get-tuple-element.109, s32[]{:T(128)S(6)} %copy.53), kind=kOutput, calls=%fused_computation.2.clone.1 | convolution fusion | flops 1511900160 | bytes 3796996 | tf_op jit(solution)/shard_map/while/body/eval_jaxpr/vmap()/dot_general | solution.py:20
  161.6 0.6 bitcast_dynamic-update-slice_fusion.2
  162.2 4.7 %log-plus-one_reduce_fusion.2 = f32[8,1920]{1,0:T(8,128)S(1)} fusion(bf16[768,1920]{1,0:T(8,128)(2,1)} %get-tuple-element.110, bf16[9,8,64,768]{3,2,1,0:T(8,128)(2,1)} %get-tuple-element.109, s32[]{:T(128)S(6)} %copy.53), kind=kOutput, calls=%fused_computation.2.clone.1 | convolution fusion | flops 1511900160 | bytes 3796996 | tf_op jit(solution)/shard_map/while/body/eval_jaxpr/vmap()/dot_general | solution.py:20
  166.9 0.6 bitcast_dynamic-update-slice_fusion.2
  167.6 4.7 %log-plus-one_reduce_fusion.2 = f32[8,1920]{1,0:T(8,128)S(1)} fusion(bf16[768,1920]{1,0:T(8,128)(2,1)} %get-tuple-element.110, bf16[9,8,64,768]{3,2,1,0:T(8,128)(2,1)} %get-tuple-element.109, s32[]{:T(128)S(6)} %copy.53), kind=kOutput, calls=%fused_computation.2.clone.1 | convolution fusion | flops 1511900160 | bytes 3796996 | tf_op jit(solution)/shard_map/while/body/eval_jaxpr/vmap()/dot_general | solution.py:20
  172.3 0.6 bitcast_dynamic-update-slice_fusion.2
  172.9 4.7 %log-plus-one_reduce_fusion.2 = f32[8,1920]{1,0:T(8,128)S(1)} fusion(bf16[768,1920]{1,0:T(8,128)(2,1)} %get-tuple-element.110, bf16[9,8,64,768]{3,2,1,0:T(8,128)(2,1)} %get-tuple-element.109, s32[]{:T(128)S(6)} %copy.53), kind=kOutput, calls=%fused_computation.2.clone.1 | convolution fusion | flops 1511900160 | bytes 3796996 | tf_op jit(solution)/shard_map/while/body/eval_jaxpr/vmap()/dot_general | solution.py:20
  178.2 4.7 %log-plus-one_reduce_fusion.2 = f32[8,1920]{1,0:T(8,128)S(1)} fusion(bf16[768,1920]{1,0:T(8,128)(2,1)} %get-tuple-element.110, bf16[9,8,64,768]{3,2,1,0:T(8,128)(2,1)} %get-tuple-element.109, s32[]{:T(128)S(6)} %copy.53), kind=kOutput, calls=%fused_computation.2.clone.1 | convolution fusion | flops 1511900160 | bytes 3796996 | tf_op jit(solution)/shard_map/while/body/eval_jaxpr/vmap()/dot_general | solution.py:20
  183.6 2.1 reshape_reshape.3
  185.7 2.5 fusion.56
  188.1 12.1 %all-reduce = f32[8,9]{1,0:T(8,128)S(1)} all-reduce(f32[8,9]{1,0:T(8,128)S(1)} %bitcast.165), channel_id=4, replica_groups=mesh['group'=4,'shard'=8] {'shard'}, use_global_device_ids=true, to_apply=%region_14.15.clone | all-reduce | flops 72 | bytes 576
  200.3 0.6 dynamic-slice_multiply_fusion
  201.0 1.4 fusion.74
  202.6 0.7 multiply_multiply_fusion.16
  203.3 0.7 subtract_multiply_fusion
  204.0 43.9 %all-gather.3 = f32[32,10,768]{2,1,0:T(8,128)} all-gather(f32[1,10,768]{2,1,0:T(8,128)S(1)} %maximum_bitcast_fusion.1), channel_id=1, replica_groups=mesh['group'=4,'shard'=8] {'group','shard'}, dimensions={0}, use_global_device_ids=true | all-gather | bytes 1013760 | tf_op jit(solution)/shard_map/all_gather | solution.py:125
  247.9 2.4 reshape.546
  250.3 6.9 %fusion.81 = f32[768,768]{1,0:T(8,128)} fusion(f32[320,768]{1,0:T(8,128)} %reshape.544, f32[320,768]{1,0:T(8,128)} %reshape.546), kind=kOutput, calls=%fused_computation.174 | convolution fusion | flops 2264924160 | bytes 4325376 | tf_op jit(solution)/shard_map/rd,re->de/dot_general | solution.py:29
  (64 shorter events, 5.5 us)
Async XLA Ops:
  7.2 12.2 %copy-start = (bf16[32,64,768]{2,1,0:T(8,128)(2,1)S(1)}, bf16[32,64,768]{2,1,0:T(8,128)(2,1)}, u32[]{:S(2)}) copy-start(bf16[32,64,768]{2,1,0:T(8,128)(2,1)} %param.12) | copy-start | bytes 9437188
  9.2 9.8 %all-to-all-start = ((s32[8,1,2]{2,1,0:T(1,128)}), s32[8,1,2]{2,1,0:T(1,128)S(1)}, u32[]{:S(2)}, u32[]{:S(2)}) async-start(s32[8,1,2]{2,1,0:T(1,128)} %copy.29), calls=%async_computation | async-start | bytes 8192 | tf_op jit(solution)/shard_map/all_to_all | solution.py:62
  14.4 121.1 %all-gather.6.cloned.1.call-start = ((), (), s32[]{:S(2)}) async-start(), calls=%async_computation.1 | async-start | bytes 7962624 | tf_op jit(solution)/shard_map/all_gather | solution.py:86
  24.0 0.8 copy-start.4
  24.8 3.6 %collective-permute-start = (bf16[1,2,64,768]{3,2,1,0:T(8,128)(2,1)S(1)}, bf16[1,2,64,768]{3,2,1,0:T(8,128)(2,1)S(1)}, u32[]{:S(2)}, u32[]{:S(2)}) collective-permute-start(bf16[1,2,64,768]{3,2,1,0:T(8,128)(2,1)S(1)} %get-tuple-element.58), channel_id=1, source_target_pairs={{0,1},{1,0},{2,3},{3,2},{4,5},{5,4},{6,7},{7,6},{8,9},{9,8},{10,11... | collective-permute-start | bytes 589832 | tf_op jit(solution)/shard_map/ppermute | solution.py:76
  24.8 7.8 %collective-permute-start.1 = (bf16[1,2,64,768]{3,2,1,0:T(8,128)(2,1)S(1)}, bf16[1,2,64,768]{3,2,1,0:T(8,128)(2,1)S(1)}, u32[]{:S(2)}, u32[]{:S(2)}) collective-permute-start(bf16[1,2,64,768]{3,2,1,0:T(8,128)(2,1)S(1)} %get-tuple-element.57), channel_id=1, source_target_pairs={{0,2},{1,3},{2,0},{3,1},{4,6},{5,7},{6,4},{7,5},{8,10},{9,11},{10,... | collective-permute-start | bytes 589832 | tf_op jit(solution)/shard_map/ppermute | solution.py:76
  25.5 10.5 %collective-permute-start.2 = (bf16[1,2,64,768]{3,2,1,0:T(8,128)(2,1)S(1)}, bf16[1,2,64,768]{3,2,1,0:T(8,128)(2,1)S(1)}, u32[]{:S(2)}, u32[]{:S(2)}) collective-permute-start(bf16[1,2,64,768]{3,2,1,0:T(8,128)(2,1)S(1)} %get-tuple-element.56), channel_id=1, source_target_pairs={{0,3},{1,2},{2,1},{3,0},{4,7},{5,6},{6,5},{7,4},{8,11},{9,10},{10,... | collective-permute-start | bytes 589832 | tf_op jit(solution)/shard_map/ppermute | solution.py:76
  26.8 9.9 %collective-permute-start.3 = (bf16[1,2,64,768]{3,2,1,0:T(8,128)(2,1)S(1)}, bf16[1,2,64,768]{3,2,1,0:T(8,128)(2,1)S(1)}, u32[]{:S(2)}, u32[]{:S(2)}) collective-permute-start(bf16[1,2,64,768]{3,2,1,0:T(8,128)(2,1)S(1)} %get-tuple-element.55), channel_id=1, source_target_pairs={{0,4},{1,5},{2,6},{3,7},{4,0},{5,1},{6,2},{7,3},{8,12},{9,13},{10,... | collective-permute-start | bytes 589832 | tf_op jit(solution)/shard_map/ppermute | solution.py:76
  27.3 18.5 %collective-permute-start.4 = (bf16[1,2,64,768]{3,2,1,0:T(8,128)(2,1)S(1)}, bf16[1,2,64,768]{3,2,1,0:T(8,128)(2,1)S(1)}, u32[]{:S(2)}, u32[]{:S(2)}) collective-permute-start(bf16[1,2,64,768]{3,2,1,0:T(8,128)(2,1)S(1)} %get-tuple-element.54), channel_id=1, source_target_pairs={{0,5},{1,4},{2,7},{3,6},{4,1},{5,0},{6,3},{7,2},{8,13},{9,12},{10,... | collective-permute-start | bytes 589832 | tf_op jit(solution)/shard_map/ppermute | solution.py:76
  28.4 18.1 %collective-permute-start.5 = (bf16[1,2,64,768]{3,2,1,0:T(8,128)(2,1)S(1)}, bf16[1,2,64,768]{3,2,1,0:T(8,128)(2,1)S(1)}, u32[]{:S(2)}, u32[]{:S(2)}) collective-permute-start(bf16[1,2,64,768]{3,2,1,0:T(8,128)(2,1)S(1)} %get-tuple-element.53), channel_id=1, source_target_pairs={{0,6},{1,7},{2,4},{3,5},{4,2},{5,3},{6,0},{7,1},{8,14},{9,15},{10,... | collective-permute-start | bytes 589832 | tf_op jit(solution)/shard_map/ppermute | solution.py:76
  32.7 14.5 %collective-permute-start.6 = (bf16[1,2,64,768]{3,2,1,0:T(8,128)(2,1)S(1)}, bf16[1,2,64,768]{3,2,1,0:T(8,128)(2,1)S(1)}, u32[]{:S(2)}, u32[]{:S(2)}) collective-permute-start(bf16[1,2,64,768]{3,2,1,0:T(8,128)(2,1)S(1)} %get-tuple-element.52), channel_id=1, source_target_pairs={{0,7},{1,6},{2,5},{3,4},{4,3},{5,2},{6,1},{7,0},{8,15},{9,14},{10,... | collective-permute-start | bytes 589832 | tf_op jit(solution)/shard_map/ppermute | solution.py:76
  58.0 1.1 copy-start.5
  58.0 3.3 %copy-start.1 = (bf16[1,32,768]{2,1,0:T(8,128)(2,1)S(1)}, bf16[1,32,768]{2,1,0:T(8,128)(2,1)}, u32[]{:S(2)}) copy-start(bf16[1,32,768]{2,1,0:T(8,128)(2,1)} %param.10) | copy-start | bytes 147460
  64.3 13.7 %copy-start.3 = (bf16[768,1920]{1,0:T(8,128)(2,1)S(1)}, bf16[768,1920]{1,0:T(8,128)(2,1)}, u32[]{:S(2)}) copy-start(bf16[768,1920]{1,0:T(8,128)(2,1)} %param.16) | copy-start | bytes 8847364
  183.6 17.4 %copy-start.2 = (s32[1,8]{1,0:T(1,128)S(1)}, s32[1,8]{1,0:T(1,128)}, u32[]{:S(2)}) copy-start(s32[1,8]{1,0:T(1,128)} %param.14) | copy-start | bytes 100
Sparse Core Ops, SparseCore 0:
  59.2 59.3 all-gather.5
